TPU v7x, 256 devices: a whole 4x4x8 slice. The times are simulated.
256 devices in a mesh: dp: 64 (over y, z, core), tensor: 4 (over x).
Axes of the slice: x: 4, y: 4, z: 8, core: 2. Of those that a mesh axis runs over, the one named last changes fastest.
Arguments:
- activations: bfloat16 [32768, 8192], P('dp', 'tensor'), may hold values from -2000 to 2000
- norm_gain: float32 [8192], replicated, may hold values from 0.5 to 12
- w_query: bfloat16 [8192, 4096], P('dp', 'tensor'), may hold values from -0.0625 to 0.0625
- w_key: bfloat16 [8192, 512], P('dp', 'tensor'), may hold values from -0.0625 to 0.0625
- w_value: bfloat16 [8192, 512], P('dp', 'tensor'), may hold values from -0.0625 to 0.0625
- lengths: int32 [128], replicated, may hold values from 128 to 256
- languages: int32 [128], replicated, may hold values from 0 to 29
- lang_caps: int32 [30], replicated, may hold values from 128 to 256
- dest_shard: int32 [128], replicated, may hold values from 0 to 63, as said below
Outputs:
- attended: bfloat16 [32768, 4096], P('dp', 'tensor')
Inputs may be any that keep to these rules, and one draw needn't show every extreme that they name: `dest_shard`: every data shard receives exactly 2 documents.
All inputs are finite; a program needn't handle non-finite values.
Results may differ from a plain program's by a relative error of at most 0.007.
The roundings to bfloat16 on the way count: a program that leaves them out, or rounds other values in their place, can miss the bound.
Values may be sent and summed in bfloat16 or wider, within the bound.
A program may use at most 128 MiB of HBM per device.

v0:
```python
import math
import jax
import jax.numpy as jnp
from jax import lax
from jax.sharding import PartitionSpec as P

HEAD_WIDTH = 128
rope_base = 500000.0
norm_eps = 1e-05


def rotary_embedding(vectors, token_positions):
    half_width = vectors.shape[-1] // 2
    steps_range = jnp.arange(half_width, dtype=jnp.float32)
    frequency = jnp.exp(steps_range * (-2.0 * math.log(rope_base) / vectors.shape[-1]))
    angles = token_positions[..., None, None] * frequency
    cosine = jnp.cos(angles)
    sine_table = jnp.sin(angles)
    first_half = vectors[..., :half_width]
    second_half = vectors[..., half_width:]
    return jnp.concatenate(
        [
            first_half * cosine - second_half * sine_table,
            second_half * cosine + first_half * sine_table,
        ],
        axis=-1,
    )


def project(source_rows, norm_gain, w_query, w_key, w_value):
    gathered = lax.all_gather(source_rows, "tensor", axis=1, tiled=True)
    widened = gathered.astype(jnp.float32)
    row_scale = lax.rsqrt(jnp.mean(widened * widened, axis=1, keepdims=True) + norm_eps)
    normed = (widened * row_scale * norm_gain).astype(jnp.bfloat16)
    pieces = (
        lax.all_gather(w_query, "dp", axis=0, tiled=True),
        lax.all_gather(w_key, "dp", axis=0, tiled=True),
        lax.all_gather(w_value, "dp", axis=0, tiled=True),
    )
    return tuple(
        (
            jnp.dot(normed, weight_piece, preferred_element_type=jnp.float32)
            for weight_piece in pieces
        )
    )


def rotate_round(query_part, key_portion, value_portion, token_positions, head_dim):
    total_rows = query_part.shape[0]
    rotated_query = rotary_embedding(
        query_part.reshape(total_rows, -1, head_dim), token_positions
    ).reshape(total_rows, -1)
    rotated_key = rotary_embedding(
        key_portion.reshape(total_rows, -1, head_dim), token_positions
    ).reshape(total_rows, -1)
    return jnp.concatenate([rotated_query, rotated_key, value_portion], axis=1).astype(jnp.bfloat16)


def attend(packed, doc_lengths, query_width, key_width, head_dim, doc_max):
    total_rows = packed.shape[0]
    doc_total = total_rows // doc_max
    value_head_rows = key_width // head_dim
    heads_per_group = query_width // key_width
    queries = packed[:, :query_width].reshape(
        doc_total, doc_max, value_head_rows, heads_per_group, head_dim
    )
    key_rows = packed[:, query_width : query_width + key_width].reshape(
        doc_total, doc_max, value_head_rows, head_dim
    )
    value_rows = packed[:, query_width + key_width :].reshape(
        doc_total, doc_max, value_head_rows, head_dim
    )
    scores = jnp.einsum(
        "jqhgd,jkhd->jhgqk", queries, key_rows, preferred_element_type=jnp.float32
    ) / math.sqrt(head_dim)
    order_range = jnp.arange(doc_max)
    causal = order_range[:, None] >= order_range[None, :]
    scores = jnp.where(causal, scores, -jnp.inf)
    row_peak = jnp.max(scores, axis=-1, keepdims=True)
    exponent = jnp.exp(scores - row_peak)
    probability = (exponent / jnp.sum(exponent, axis=-1, keepdims=True)).astype(jnp.bfloat16)
    blended = jnp.einsum(
        "jhgqk,jkhd->jqhgd", probability, value_rows, preferred_element_type=jnp.float32
    )
    blended = blended.reshape(doc_total, doc_max, query_width)
    row_valid = order_range[None, :] < doc_lengths[:, None]
    result = jnp.where(row_valid[..., None], blended, 0.0)
    return result.reshape(total_rows, query_width).astype(jnp.bfloat16)


def local(
    activations, norm_gain, w_query, w_key, w_value, lengths, languages, lang_caps, dest_shard
):
    shard_count = lax.axis_size("dp")
    my_shard = lax.axis_index("dp")
    doc_count = lengths.shape[0]
    token_rows = activations.shape[0]
    rows_peer = token_rows // doc_count
    doc_max = rows_peer * shard_count
    docs_here = doc_count // shard_count
    head_dim = HEAD_WIDTH
    query_width = w_query.shape[1]
    key_width = w_key.shape[1]
    language_table = jnp.arange(lang_caps.shape[0])
    cap_of_doc = jnp.sum(
        jnp.where(languages[:, None] == language_table[None, :], lang_caps[None, :], 0), axis=1
    )
    capped = jnp.minimum(lengths, cap_of_doc)
    doc_order = jnp.arange(doc_count)
    same_dest = dest_shard[:, None] == dest_shard[None, :]
    doc_rank = jnp.sum(
        (same_dest & (doc_order[None, :] < doc_order[:, None])).astype(jnp.int32), axis=1
    )
    target_slot = dest_shard * docs_here + doc_rank
    holder = jnp.sum(
        jnp.where(doc_order[:, None] == target_slot[None, :], doc_order[None, :], 0), axis=1
    )
    mine = lax.dynamic_slice_in_dim(holder, my_shard * docs_here, docs_here)
    doc_lengths = jnp.take(capped, mine)
    holder_grid = jnp.transpose(holder.reshape(shard_count, docs_here))
    send_index = (
        holder_grid[:, None, :] * rows_peer + jnp.arange(rows_peer)[None, :, None]
    ).reshape(-1)
    outgoing = jnp.take(activations, send_index, axis=0).reshape(
        docs_here, rows_peer, shard_count, -1
    )
    arrived = lax.all_to_all(outgoing, "dp", split_axis=2, concat_axis=2, tiled=True)
    moved_rows = arrived.reshape(docs_here * doc_max, -1)
    query_part, key_portion, value_portion = project(moved_rows, norm_gain, w_query, w_key, w_value)
    token_positions = jnp.tile(jnp.arange(doc_max), docs_here).astype(jnp.float32)
    packed = rotate_round(query_part, key_portion, value_portion, token_positions, head_dim)
    return attend(packed, doc_lengths, query_width, key_width, head_dim, doc_max)


def solution(mesh):
    return jax.shard_map(
        local,
        mesh=mesh,
        in_specs=(
            P("dp", "tensor"),
            P(),
            P("dp", "tensor"),
            P("dp", "tensor"),
            P("dp", "tensor"),
            P(),
            P(),
            P(),
            P(),
        ),
        out_specs=P("dp", "tensor"),
        check_vma=False,
    )
```

profile of v0, /device:TPU:1, one launch (start us, length us, event | category | flops | bytes accessed | tf_op | source)
XLA Modules:
  0.0 453.7 jit_solution(18384676850716704676)
XLA Ops:
  6.5 0.0 copy-start
  6.5 0.0 all-gather.5.cloned.1.call-start
  6.5 1.0 convert_reduce_fusion
  7.5 0.7 multiply_add_fusion
  8.2 0.1 select_reduce_fusion
  8.3 0.1 mul.188
  8.5 0.1 copy.35
  8.6 0.1 add.84
  8.7 0.1 copy.36
  8.8 0.0 copy-done
  8.8 3.3 gather_fusion.1
  12.2 3.8 copy_select_fusion
  16.0 64.1 %all_to_all.5 = bf16[2,4,64,2048]{3,1,0,2:T(4,128)(2,1)S(1)} all-to-all(bf16[2,4,64,2048]{3,1,0,2:T(4,128)(2,1)S(1)} %copy_select_fusion), channel_id=1, replica_groups=mesh['dp'=64,'tensor'=4] {'dp'}, dimensions={2} | all-to-all | bytes 4194304 | tf_op jit(solution)/shard_map/all_to_all | solution.py:127
  80.1 2.5 copy.38
  82.7 0.0 all-gather.5.cloned.1.call-update
  82.7 0.0 all-gather.9.cloned.1.call-start
  82.7 0.7 all-gather.9.cloned.1.call-update
  83.4 0.0 all-gather.7.cloned.1.call-start
  83.5 0.7 all-gather.7.cloned.1.call-update
  84.2 0.0 all-gather.11.cloned.1.call-start
  84.2 0.5 all-gather.11.cloned.1.call-update
  84.8 0.0 copy-done.2
  84.8 0.0 copy-done.3
  84.8 0.1 select_reduce_fusion.1
  84.9 0.1 compare_select_fusion.2
  85.0 0.6 gather_fusion
  85.6 0.1 and_select_fusion
  85.7 0.1 iota_compare_fusion.4
  85.8 1.0 multiply_cosine_fusion
  86.8 0.0 copy-start.1
  86.8 77.9 %all-gather.5.cloned.1.call-done = bf16[512,8192]{1,0:T(8,128)(2,1)} async-done(((bf16[512,2048]{1,0:T(8,128)(2,1)}), bf16[512,8192]{1,0:T(8,128)(2,1)}) %all-gather.5.cloned.1.call-update) | async-done | bytes 8388624 | tf_op jit(solution)/shard_map/all_gather | solution.py:31
  164.7 5.1 %fusion = f32[512]{0:T(512)S(1)} fusion(bf16[512,8192]{1,0:T(8,128)(2,1)} %all-gather.5.cloned.1.call-done), kind=kLoop, calls=%fused_computation.4 | loop fusion | flops 12582400 | bytes 8390656 | tf_op jit(solution)/shard_map/reduce_sum | solution.py:33
  169.8 76.8 %all-gather.9.cloned.1.call-done = bf16[8192,128]{1,0:T(8,128)(2,1)} async-done(((bf16[128,128]{1,0:T(8,128)(2,1)}), bf16[8192,128]{1,0:T(8,128)(2,1)}) %all-gather.9.cloned.1.call-update) | async-done | bytes 2097168 | tf_op jit(solution)/shard_map/all_gather | solution.py:37
  246.6 6.5 %convolution_bitcast_fusion.1 = f32[512,1,128]{0,2,1:T(8,128)S(1)} fusion(bf16[8192,128]{1,0:T(8,128)(2,1)} %all-gather.9.cloned.1.call-done, bf16[512,8192]{1,0:T(8,128)(2,1)} %all-gather.5.cloned.1.call-done, f32[8192]{0:T(1024)S(1)} %copy-done.1, f32[512]{0:T(512)S(1)} %add_rsqrt_fusion), kind=kOutput, calls=%fused_computation.22 | convolution fusion | flops 1090519040 | bytes 10782720 | tf_op jit(solution)/shard_map/dot_general | solution.py:42
  253.1 0.6 fusion.19
  253.7 0.1 copy.49
  253.8 70.6 %all-gather.7.cloned.1.call-done = bf16[8192,128]{1,0:T(8,128)(2,1)} async-done(((bf16[128,128]{1,0:T(8,128)(2,1)}), bf16[8192,128]{1,0:T(8,128)(2,1)}) %all-gather.7.cloned.1.call-update) | async-done | bytes 2097168 | tf_op jit(solution)/shard_map/all_gather | solution.py:38
  324.4 6.4 %convolution_convert_fusion = bf16[512,128]{1,0:T(8,128)(2,1)S(1)} fusion(bf16[8192,128]{1,0:T(8,128)(2,1)} %all-gather.7.cloned.1.call-done, bf16[512,8192]{1,0:T(8,128)(2,1)} %all-gather.5.cloned.1.call-done, f32[8192]{0:T(1024)S(1)} %copy-done.1, f32[512]{0:T(512)S(1)} %add_rsqrt_fusion), kind=kOutput, calls=%fused_computation.23 | convolution fusion | flops 1090584576 | bytes 10651648 | tf_op jit(solution)/shard_map/dot_general | solution.py:42
  330.8 93.0 %all-gather.11.cloned.1.call-done = bf16[8192,1024]{1,0:T(8,128)(2,1)} async-done(((bf16[128,1024]{1,0:T(8,128)(2,1)}), bf16[8192,1024]{1,0:T(8,128)(2,1)}) %all-gather.11.cloned.1.call-update) | async-done | bytes 16777232 | tf_op jit(solution)/shard_map/all_gather | solution.py:36
  423.8 14.5 %convolution_bitcast_fusion = f32[64,8,8,128]{3,1,2,0:T(8,128)S(1)} fusion(bf16[8192,1024]{1,0:T(8,128)(2,1)} %all-gather.11.cloned.1.call-done, bf16[512,8192]{1,0:T(8,128)(2,1)} %all-gather.5.cloned.1.call-done, f32[8192]{0:T(1024)S(1)} %copy-done.1, f32[512]{0:T(512)S(1)} %add_rsqrt_fusion), kind=kOutput, calls=%fused_computation.21 | convolution fusion | flops 8606711808 | bytes 27297792 | tf_op jit(solution)/shard_map/dot_general | solution.py:42
  438.3 0.5 copy.51
  438.8 0.9 subtract_convert_fusion
  439.7 0.6 pad_maximum_fusion
  440.3 0.8 fusion.4
  441.0 0.9 fusion.3
  441.9 2.3 fusion.9
  444.2 1.7 copy.43
  445.9 1.2 fusion.5
  (19 shorter events, 0.2 us)
Async XLA Ops:
  6.5 2.3 copy-start
  6.5 158.2 %all-gather.5.cloned.1.call-start = ((), (), s32[]{:S(2)}) async-start(), calls=%async_computation.1 | async-start | bytes 10485760 | tf_op jit(solution)/shard_map/all_gather | solution.py:31
  80.1 4.6 %copy-start.2 = (s32[30]{0:T(128)S(1)}, s32[30]{0:T(128)}, u32[]{:S(2)}) copy-start(s32[30]{0:T(128)} %param.16) | copy-start | bytes 364
  80.1 4.6 %copy-start.3 = (s32[128]{0:T(128)S(1)}, s32[128]{0:T(128)}, u32[]{:S(2)}) copy-start(s32[128]{0:T(128)} %param.15) | copy-start | bytes 1540
  80.1 4.7 %copy-start.4 = (s32[128]{0:T(128)S(1)}, s32[128]{0:T(128)}, u32[]{:S(2)}) copy-start(s32[128]{0:T(128)} %param.14) | copy-start | bytes 1540
  82.7 164.0 %all-gather.9.cloned.1.call-start = ((), (), s32[]{:S(2)}) async-start(), calls=%async_computation.3 | async-start | bytes 2129920 | tf_op jit(solution)/shard_map/all_gather | solution.py:37
  83.4 241.0 %all-gather.7.cloned.1.call-start = ((), (), s32[]{:S(2)}) async-start(), calls=%async_computation.2 | async-start | bytes 2129920 | tf_op jit(solution)/shard_map/all_gather | solution.py:38
  84.2 339.6 %all-gather.11.cloned.1.call-start = ((), (), s32[]{:S(2)}) async-start(), calls=%async_computation.4 | async-start | bytes 17039360 | tf_op jit(solution)/shard_map/all_gather | solution.py:36
  86.8 159.8 %copy-start.1 = (f32[8192]{0:T(1024)S(1)}, f32[8192]{0:T(1024)}, u32[]{:S(2)}) copy-start(f32[8192]{0:T(1024)} %param.10) | copy-start | bytes 98308
Sparse Core Ops, SparseCore 0:
  82.8 81.8 all-gather.4
  167.5 79.0 all-gather.8
  249.4 74.9 all-gather.6
  327.1 96.6 all-gather.10
where the time goes:
time: 454 us
  waiting for transfers between devices  320 us (70%)
  blocking collectives  64.1 us (14%)
  matrix products  30.4 us (7%)
  other arithmetic  16.2 us (4%)
  between operations  13.3 us (3%)
  local copies, waits for them, and re-layouts  9.25 us (2%)
    all_gather x1, waiting for transfers between devices, project(): lax.all_gather(w_query, 'dp', axis=0, tiled=True)  93 us
    all_gather x1, waiting for transfers between devices, project(): gathered = lax.all_gather(source_rows, 'tensor', axis=1, tiled=True)  77.9 us
    all_gather x1, waiting for transfers between devices, project(): lax.all_gather(w_key, 'dp', axis=0, tiled=True)  76.8 us
    all_gather x1, waiting for transfers between devices, project(): lax.all_gather(w_value, 'dp', axis=0, tiled=True)  70.6 us
    all_to_all x1, blocking collectives, local(): lax.all_to_all(outgoing, 'dp', split_axis=2, concat_axis=2, tiled=True)  64.1 us
    dot_general x3, matrix products, project(): jnp.dot(normed, weight_piece, preferred_element_type=jnp.float32)  27.4 us
  transfers between devices with their start and end apart: 4, of which 4 were waited for; matrix products, arithmetic and copies ran while one was open for 5% of the time, Pallas kernels for 0%

commit v1 on v0

--- a/solution.py
+++ b/solution.py
@@ -1,3 +1,4 @@
+import functools
 import math
 import jax
 import jax.numpy as jnp
@@ -7,6 +8,35 @@
 HEAD_WIDTH = 128
 rope_base = 500000.0
 norm_eps = 1e-05
+
+
+def link_local_data(matrix, along_dim):
+    matrix = jnp.moveaxis(matrix, 0, along_dim)
+    r1 = matrix.shape
+    return matrix.reshape(*r1[:along_dim], r1[along_dim] * r1[along_dim + 1], *r1[along_dim + 2 :])
+
+
+def bring_local_data_on_mesh(piece_in, link_axis, in_dim):
+    width = lax.axis_size(link_axis)
+    kept_rows = list(map(lambda dev_j: (dev_j, (dev_j + 1) % width), range(width)))
+    row_list = [(kk, num) for num, kk in kept_rows]
+    then, v_next = ([], [])
+    for dev in range(width - 1):
+        if dev % 2 == 0:
+            piece_now = lax.ppermute(then[-1] if then else piece_in, link_axis, kept_rows)
+            then.append(piece_now)
+        else:
+            v_next.append(
+                lax.ppermute(v_next[-1] if v_next else piece_in, axis_name=link_axis, perm=row_list)
+            )
+    raw_out = jnp.stack([*then[::-1], piece_in, *v_next])
+    aux = lax.axis_index(link_axis)
+    far_arr = aux - len(then)
+    raw_out = raw_out[(jnp.arange(width) - far_arr) % width]
+    return link_local_data(raw_out, in_dim)
+
+
+ports_edit = functools.partial(bring_local_data_on_mesh, link_axis="tensor", in_dim=1)
 
 
 def rotary_embedding(vectors, token_positions):
@@ -28,7 +58,7 @@
 
 
 def project(source_rows, norm_gain, w_query, w_key, w_value):
-    gathered = lax.all_gather(source_rows, "tensor", axis=1, tiled=True)
+    gathered = ports_edit(source_rows)
     widened = gathered.astype(jnp.float32)
     row_scale = lax.rsqrt(jnp.mean(widened * widened, axis=1, keepdims=True) + norm_eps)
     normed = (widened * row_scale * norm_gain).astype(jnp.bfloat16)

time: 454 us -> 330 us (0.73)
  waiting for transfers between devices: 320 us -> 93.3 us
  local copies, waits for them, and re-layouts: 9.25 us -> 71.9 us
  other arithmetic: 16.2 us -> 48.1 us
    all_gather x1, waiting for transfers between devices: 93 us -> 0.02 us  [project(): lax.all_gather(w_query, 'dp', axis=0, tiled=True)]
    ppermute x0 -> x3, waiting for transfers between devices: none -> 91.1 us  [the longest x2 91.1 us: bring_local_data_on_mesh(): lax.ppermute(then[-1] if then else piece_in, link_axis, kept_rows)]
    all_gather x1 -> x0, waiting for transfers between devices: 77.9 us -> none  [project(): gathered = lax.all_gather(source_rows, 'tensor', axis=1, tiled=True)]
    all_gather x1, waiting for transfers between devices: 76.8 us -> 0.01 us  [project(): lax.all_gather(w_key, 'dp', axis=0, tiled=True)]
    all_gather x1, waiting for transfers between devices: 70.6 us -> 0.01 us  [project(): lax.all_gather(w_value, 'dp', axis=0, tiled=True)]
    dot_general x0 -> x1, local copies, waits for them, and re-layouts: none -> 21.3 us  [project(): jnp.dot(normed, weight_piece, preferred_element_type=jnp.float32)]
    convert_element_type x0 -> x2, other arithmetic: none -> 20.8 us  [the longest x1 11.3 us: project(): widened = gathered.astype(jnp.float32)]
    convert_element_type x0 -> x1, local copies, waits for them, and re-layouts: none -> 16.4 us  [project(): widened = gathered.astype(jnp.float32)]
  transfers between devices with their start and end apart: 4 -> 6, of which waited for: 4 -> 2; matrix products, arithmetic and copies ran while one was open for 5% -> 33% of each run, Pallas kernels for 0% -> 0%
where the time goes in v1:
time: 330 us; the launch traced here: 327 us
  waiting for transfers between devices  93.3 us (28%)
  local copies, waits for them, and re-layouts  71.9 us (22%)
  blocking collectives  68.2 us (21%)
  other arithmetic  48.1 us (15%)
  matrix products  29.4 us (9%)
  between operations  13.4 us (4%)
    ppermute x2, waiting for transfers between devices, bring_local_data_on_mesh(): lax.ppermute(then[-1] if then else piece_in, link_axis, kept_rows)  91.1 us
    all_to_all x1, blocking collectives, local(): lax.all_to_all(outgoing, 'dp', split_axis=2, concat_axis=2, tiled=True)  68.2 us
    dot_general x3, matrix products, project(): jnp.dot(normed, weight_piece, preferred_element_type=jnp.float32)  26.4 us
    dot_general x1, local copies, waits for them, and re-layouts, project(): jnp.dot(normed, weight_piece, preferred_element_type=jnp.float32)  21.3 us
    convert_element_type x1, local copies, waits for them, and re-layouts, project(): widened = gathered.astype(jnp.float32)  16.4 us
    gather x3, local copies, waits for them, and re-layouts, bring_local_data_on_mesh(): raw_out = raw_out[(jnp.arange(width) - far_arr) % width]  13.9 us
    mul x2, local copies, waits for them, and re-layouts, project(): normed = (widened * row_scale * norm_gain).astype(jnp.bfloat16)  11.5 us
    convert_element_type x1, other arithmetic, project(): widened = gathered.astype(jnp.float32)  11.3 us
  transfers between devices with their start and end apart: 6, of which 2 were waited for; matrix products, arithmetic and copies ran while one was open for 33% of the time, Pallas kernels for 0%

profile of v1, /device:TPU:1, one launch (start us, length us, event | category | flops | bytes accessed | tf_op | source)
XLA Modules:
  0.0 327.0 jit_solution(1093485672830293112)
XLA Ops:
  6.5 0.7 all-gather.6.cloned.1.call-update
  7.3 0.7 all-gather.4.cloned.1.call-update
  8.1 0.7 all-gather.8.cloned.1.call-update
  8.7 0.9 convert_reduce_fusion
  9.6 0.7 multiply_add_fusion
  10.3 0.1 select_reduce_fusion
  10.4 0.1 mul.206
  10.6 0.1 copy.59
  10.7 0.1 add.108
  10.8 0.1 copy.60
  11.0 3.3 %gather_fusion.1 = bf16[512,2048]{1,0:T(8,128)(2,1)} fusion(bf16[512,2048]{1,0:T(8,128)(2,1)S(1)} %copy-done, s32[1024]{0:T(1024)S(1)} %pad_clamp_fusion.1), kind=kCustom, calls=%fused_computation.1 | custom fusion | bytes 4196352 | tf_op jit(solution)/shard_map/jit(_take)/gather | solution.py:154
  14.3 3.8 %copy_select_fusion = bf16[2,4,64,2048]{3,1,0,2:T(4,128)(2,1)S(1)} fusion(bf16[2,4,64,2048]{3,2,1,0:T(8,128)(2,1)} %bitcast.87, pred[2,4,64]{1,0,2:T(4,128)(4,1)S(1)} %copy.60), kind=kLoop, calls=%fused_computation.25 | loop fusion | flops 1048576 | bytes 4194816 | tf_op jit(solution)/shard_map/jit(_take)/select_n | solution.py:154
  18.2 68.2 %all_to_all.5 = bf16[2,4,64,2048]{3,1,0,2:T(4,128)(2,1)S(1)} all-to-all(bf16[2,4,64,2048]{3,1,0,2:T(4,128)(2,1)S(1)} %copy_select_fusion), channel_id=1, replica_groups=mesh['dp'=64,'tensor'=4] {'dp'}, dimensions={2} | all-to-all | bytes 4194304 | tf_op jit(solution)/shard_map/all_to_all | solution.py:157
  86.4 2.5 copy.62
  88.9 1.3 collective-permute-start
  90.1 1.4 collective-permute-start.2
  91.5 45.6 %collective-permute-done = bf16[512,2048]{1,0:T(8,128)(2,1)} collective-permute-done((bf16[512,2048]{1,0:T(8,128)(2,1)}, bf16[512,2048]{1,0:T(8,128)(2,1)}, u32[]{:S(2)}, u32[]{:S(2)}) %collective-permute-start) | collective-permute-done | bytes 2097184 | tf_op jit(solution)/shard_map/ppermute | solution.py:26
  137.1 0.1 collective-permute-start.1
  137.3 0.1 select_reduce_fusion.1
  137.4 0.1 compare_select_fusion.3
  137.5 0.6 gather_fusion
  138.1 0.1 and_select_fusion.1
  138.2 0.1 iota_compare_fusion.4
  138.4 0.5 multiply_cosine_fusion
  138.9 45.6 %collective-permute-done.1 = bf16[512,2048]{1,0:T(8,128)(2,1)} collective-permute-done((bf16[512,2048]{1,0:T(8,128)(2,1)}, bf16[512,2048]{1,0:T(8,128)(2,1)}, u32[]{:S(2)}, u32[]{:S(2)}) %collective-permute-start.1) | collective-permute-done | bytes 2097184 | tf_op jit(solution)/shard_map/ppermute | solution.py:26
  184.5 4.5 %pad_maximum_fusion = bf16[4,512,2048]{2,1,0:T(8,128)(2,1)S(1)} fusion(bf16[1,512,2048]{2,1,0:T(8,128)(2,1)} %bitcast.7, bf16[1,512,2048]{2,1,0:T(8,128)(2,1)} %bitcast.6, bf16[1,512,2048]{2,1,0:T(8,128)(2,1)} %bitcast.5, bf16[1,512,2048]{2,1,0:T(8,128)(2,1)} %bitcast.4), kind=kLoop, calls=%fused_computation.14 | loop fusion | flops 12582912 | bytes 16777216 | tf_op jit(solution)/shard_map/stack | solution.py:32
  189.0 3.8 %fusion.31 = (bf16[4,512,1024]{2,1,0:T(8,128)(2,1)}, bf16[4,512,1024]{2,1,0:T(8,128)(2,1)}) fusion(bf16[4,512,2048]{2,1,0:T(8,128)(2,1)S(1)} %pad_maximum_fusion), kind=kLoop, calls=%fused_computation.80 | loop fusion | bytes 16777216 | tf_op jit(solution)/shard_map/gather | solution.py:35
  192.8 5.0 %gather_fusion.3 = bf16[4,512,1024]{2,1,0:T(8,128)(2,1)} fusion(bf16[4,512,1024]{2,1,0:T(8,128)(2,1)} %get-tuple-element.6, s32[1024]{0:T(1024)S(1)} %pad_clamp_fusion), kind=kCustom, calls=%fused_computation.3 | custom fusion | bytes 8388624 | tf_op jit(solution)/shard_map/gather | solution.py:35
  197.9 5.0 %gather_fusion.2 = bf16[4,512,1024]{2,1,0:T(8,128)(2,1)} fusion(bf16[4,512,1024]{2,1,0:T(8,128)(2,1)} %get-tuple-element.5, s32[1024]{0:T(1024)S(1)} %pad_clamp_fusion), kind=kCustom, calls=%fused_computation.2 | custom fusion | bytes 8388624 | tf_op jit(solution)/shard_map/gather | solution.py:35
  202.9 11.3 %convert_bitcast_fusion = f32[512,4,2048]{2,0,1:T(8,128)} fusion(bf16[4,512,1024]{2,1,0:T(8,128)(2,1)} %gather_fusion.3, bf16[4,512,1024]{2,1,0:T(8,128)(2,1)} %gather_fusion.2), kind=kLoop, calls=%fused_computation.6 | loop fusion | flops 16777216 | bytes 25165824 | tf_op jit(solution)/shard_map/convert_element_type | solution.py:62
  214.2 16.4 %copy.64 = f32[512,4,2048]{0,2,1:T(8,128)} copy(f32[512,4,2048]{2,0,1:T(8,128)} %convert_bitcast_fusion) | data formatting | bytes 33554432 | tf_op jit(solution)/shard_map/convert_element_type | solution.py:62
  230.6 5.1 %fusion = f32[512]{0:T(512)S(1)} fusion(bf16[4,512,1024]{2,1,0:T(8,128)(2,1)} %gather_fusion.3, bf16[4,512,1024]{2,1,0:T(8,128)(2,1)} %gather_fusion.2), kind=kLoop, calls=%fused_computation.7 | loop fusion | flops 25165312 | bytes 8390656 | tf_op jit(solution)/shard_map/reduce_sum | solution.py:63
  235.7 9.5 %fusion.4 = bf16[512,8192]{0,1:T(8,128)(2,1)} fusion(f32[512,4,2048]{0,2,1:T(8,128)} %copy.64, f32[8192]{0:T(1024)S(1)} %copy-done.2, f32[512]{0:T(512)S(1)} %add_rsqrt_fusion), kind=kLoop, calls=%fused_computation.12 | loop fusion | flops 12582912 | bytes 25200640 | tf_op jit(solution)/shard_map/convert_element_type | solution.py:64
  245.3 5.8 %convolution_bitcast_fusion = f32[512,1,128]{0,2,1:T(8,128)S(1)} fusion(bf16[512,8192]{0,1:T(8,128)(2,1)} %fusion.4, bf16[8192,128]{1,0:T(8,128)(2,1)} %all-gather.6.cloned.1.call-done), kind=kOutput, calls=%fused_computation.28 | convolution fusion | flops 1073741824 | bytes 10747904 | tf_op jit(solution)/shard_map/dot_general | solution.py:72
  251.0 0.6 fusion.23
  251.6 0.1 copy.79
  251.7 8.1 %fusion.5 = bf16[512,4,2048]{2,0,1:T(8,128)(2,1)} fusion(f32[4,2048]{1,0:T(4,128)S(1)} %mul.223, f32[512]{0:T(512)S(1)} %add_rsqrt_fusion, bf16[4,512,1024]{2,1,0:T(8,128)(2,1)} %gather_fusion.3, bf16[4,512,1024]{2,1,0:T(8,128)(2,1)} %gather_fusion.2), kind=kLoop, calls=%fused_computation.13 | loop fusion | flops 29360128 | bytes 16812032 | tf_op jit(solution)/shard_map/mul | solution.py:64
  259.8 11.5 %copy.65 = bf16[512,4,2048]{0,2,1:T(8,128)(2,1)} copy(bf16[512,4,2048]{2,0,1:T(8,128)(2,1)} %fusion.5) | data formatting | bytes 16777216 | tf_op jit(solution)/shard_map/mul | solution.py:64
  271.4 6.4 %convolution_convert_fusion = bf16[512,128]{1,0:T(8,128)(2,1)S(1)} fusion(bf16[512,8192]{0,1:T(8,128)(2,1)} %fusion.4, bf16[8192,128]{1,0:T(8,128)(2,1)} %all-gather.4.cloned.1.call-done), kind=kOutput, calls=%fused_computation.29 | convolution fusion | flops 1073807360 | bytes 10616832 | tf_op jit(solution)/shard_map/dot_general | solution.py:72
  277.8 21.3 %copy.66 = bf16[1024,8192]{1,0:T(8,128)(2,1)} copy(bf16[1024,8192]{0,1:T(8,128)(2,1)} %bitcast.85) | data formatting | bytes 33554432 | tf_op jit(solution)/shard_map/dot_general | solution.py:72
  299.0 14.2 %fusion.32 = f32[512,8,128]{0,2,1:T(8,128)S(1)} fusion(bf16[512,8192,1]{0,1,2:T(8,128)(2,1)} %bitcast.88, bf16[8,128,8192]{2,1,0:T(8,128)(2,1)} %bitcast.86), kind=kOutput, calls=%fused_computation.81 | convolution fusion | flops 8589934592 | bytes 27262976 | tf_op jit(solution)/shard_map/dot_general | solution.py:72
  313.3 0.3 subtract_convert_fusion
  313.6 0.1 pad_maximum_fusion.2
  313.7 0.7 fusion.7
  314.4 0.9 fusion.6
  315.3 2.3 fusion.12
  317.6 1.7 copy.72
  319.3 1.2 fusion.8
  (36 shorter events, 0.3 us)
Async XLA Ops:
  6.5 4.4 %copy-start = (bf16[512,2048]{1,0:T(8,128)(2,1)S(1)}, bf16[512,2048]{1,0:T(8,128)(2,1)}, u32[]{:S(2)}) copy-start(bf16[512,2048]{1,0:T(8,128)(2,1)} %param.9) | copy-start | bytes 6291460
  6.5 238.7 %all-gather.6.cloned.1.call-start = ((), (), s32[]{:S(2)}) async-start(), calls=%async_computation.2 | async-start | bytes 2129920 | tf_op jit(solution)/shard_map/all_gather | solution.py:67
  7.3 264.1 %all-gather.4.cloned.1.call-start = ((), (), s32[]{:S(2)}) async-start(), calls=%async_computation.1 | async-start | bytes 2129920 | tf_op jit(solution)/shard_map/all_gather | solution.py:68
  8.0 269.7 %all-gather.8.cloned.1.call-start = ((), (), s32[]{:S(2)}) async-start(), calls=%async_computation.3 | async-start | bytes 17039360 | tf_op jit(solution)/shard_map/all_gather | solution.py:66
  18.1 119.1 %copy-start.2 = (f32[8192]{0:T(1024)S(1)}, f32[8192]{0:T(1024)}, u32[]{:S(2)}) copy-start(f32[8192]{0:T(1024)} %param.10) | copy-start | bytes 98308
  18.1 119.1 %copy-start.3 = (s32[30]{0:T(128)S(1)}, s32[30]{0:T(128)}, u32[]{:S(2)}) copy-start(s32[30]{0:T(128)} %param.16) | copy-start | bytes 364
  18.1 119.1 %copy-start.4 = (s32[128]{0:T(128)S(1)}, s32[128]{0:T(128)}, u32[]{:S(2)}) copy-start(s32[128]{0:T(128)} %param.15) | copy-start | bytes 1540
  18.2 119.2 %copy-start.5 = (s32[128]{0:T(128)S(1)}, s32[128]{0:T(128)}, u32[]{:S(2)}) copy-start(s32[128]{0:T(128)} %param.14) | copy-start | bytes 1540
  88.9 48.2 %collective-permute-start = (bf16[512,2048]{1,0:T(8,128)(2,1)}, bf16[512,2048]{1,0:T(8,128)(2,1)}, u32[]{:S(2)}, u32[]{:S(2)}) collective-permute-start(bf16[512,2048]{1,0:T(8,128)(2,1)} %bitcast.3), channel_id=1, source_target_pairs={{0,1},{1,2},{2,3},{3,0},{4,5},{5,6},{6,7},{7,4},{8,9},{9,10},{10,1... | collective-permute-start | bytes 6291464 | tf_op jit(solution)/shard_map/ppermute | solution.py:26
  90.1 48.8 %collective-permute-start.2 = (bf16[512,2048]{1,0:T(8,128)(2,1)}, bf16[512,2048]{1,0:T(8,128)(2,1)}, u32[]{:S(2)}, u32[]{:S(2)}) collective-permute-start(bf16[512,2048]{1,0:T(8,128)(2,1)} %bitcast.3), channel_id=1, source_target_pairs={{1,0},{2,1},{3,2},{0,3},{5,4},{6,5},{7,6},{4,7},{9,8},{10,9},{11,1... | collective-permute-start | bytes 6291464 | tf_op jit(solution)/shard_map/ppermute | solution.py:30
  137.1 47.4 %collective-permute-start.1 = (bf16[512,2048]{1,0:T(8,128)(2,1)}, bf16[512,2048]{1,0:T(8,128)(2,1)}, u32[]{:S(2)}, u32[]{:S(2)}) collective-permute-start(bf16[512,2048]{1,0:T(8,128)(2,1)} %collective-permute-done), channel_id=1, source_target_pairs={{0,1},{1,2},{2,3},{3,0},{4,5},{5,6},{6,7},{7,4},{8,9},{9,10},{10,1... | collective-permute-start | bytes 6291464 | tf_op jit(solution)/shard_map/ppermute | solution.py:26
  315.3 5.2 %copy-start.1 = (bf16[512,2048]{1,0:T(8,128)(2,1)S(1)}, bf16[512,2048]{1,0:T(8,128)(2,1)}, u32[]{:S(2)}) copy-start(bf16[512,2048]{1,0:T(8,128)(2,1)} %param.9) | copy-start | bytes 6291460
Sparse Core Ops, SparseCore 0:
  10.1 84.4 all-gather.5
  97.3 76.1 all-gather.3
  176.3 96.6 all-gather.7
